TPU v7x, 32 devices: a whole 2x2x4 slice. The times are simulated.
32 devices in a mesh: gx: 8 (over y, x, core), row: 4 (over z).
Axes of the slice: x: 2, y: 2, z: 4, core: 2. Of those that a mesh axis runs over, the one named last changes fastest.
Arguments:
- amplitudes: float32 [128, 4096], P('gx', 'row'), may hold values from -6 to 6
- integrals: float32 [4096, 16384], P('row', 'gx'), may hold values from -0.1875 to 0.1875
- cd_irrep: int32 [32], P('row'), may hold values from 0 to 7
- ab_irrep: int32 [128], P('gx'), may hold values from 0 to 7
- allowed: int32 [8, 8], replicated, may hold values 0 or 1
- pair_occ: int32 [128, 2], P(('gx', 'row')), may hold values from 0 to 99
- occ_energy: float32 [100], replicated, may hold values from -1 to -0.25
- ab_energy: float32 [16384], replicated, may hold values from 1 to 4
Outputs:
- residual: float32 [128, 16384], P(('gx', 'row'))
- update: float32 [128, 16384], P(('gx', 'row'))
All inputs are finite; a program needn't handle non-finite values.
Results may differ from a plain program's by a relative error of at most 0.000071.
Values sent between devices are 32-bit elements; how exact they have to be, the bound alone decides.
A program may use at most 128 MiB of HBM per device.

v0:
```python
import jax
import jax.numpy as jnp
from jax import lax
from jax.sharding import PartitionSpec as P

BLK = 128


def body(amplitudes, integrals, cd_irrep, ab_irrep, allowed, pair_occ, occ_energy, ab_energy):
    irrep_labels = jnp.arange(allowed.shape[0], dtype=jnp.int32)
    cd_onehot = (cd_irrep[:, None] == irrep_labels[None, :]).astype(jnp.float32)
    ab_onehot = (ab_irrep[:, None] == irrep_labels[None, :]).astype(jnp.float32)
    irrep_table = allowed.astype(jnp.float32)
    block_mask = jnp.dot(
        jnp.dot(cd_onehot, irrep_table, precision=lax.Precision.HIGHEST),
        ab_onehot.T,
        precision=lax.Precision.HIGHEST,
    )
    cd_rows, ab_cols = integrals.shape
    effective = (
        integrals.reshape(cd_rows // BLK, BLK, ab_cols // BLK, BLK) * block_mask[:, None, :, None]
    ).reshape(cd_rows, ab_cols)
    partial_value = jnp.dot(
        lax.all_gather(amplitudes, "gx", axis=0, tiled=True),
        effective,
        precision=lax.Precision.HIGHEST,
        preferred_element_type=jnp.float32,
    )
    arrived = lax.all_to_all(partial_value, "gx", split_axis=0, concat_axis=1, tiled=True)
    residual = lax.psum_scatter(arrived, "row", scatter_dimension=0, tiled=True)
    occ_labels = jnp.arange(occ_energy.shape[0], dtype=jnp.int32)
    pair_onehot = (pair_occ[:, :, None] == occ_labels[None, None, :]).astype(jnp.float32)
    pair_energy = jnp.sum(pair_onehot * occ_energy[None, None, :], axis=(1, 2))
    update = residual / (ab_energy[None, :] - pair_energy[:, None])
    return (residual, update)


def solution(mesh):
    return jax.shard_map(
        body,
        mesh=mesh,
        in_specs=(
            P("gx", "row"),
            P("row", "gx"),
            P("row"),
            P("gx"),
            P(),
            P(("gx", "row"), None),
            P(),
            P(),
        ),
        out_specs=(P(("gx", "row"), None), P(("gx", "row"), None)),
        check_vma=False,
    )
```

profile of v0, /device:TPU:0, one launch (start us, length us, event | category | flops | bytes accessed | tf_op | source)
XLA Modules:
  0.0 108.6 jit_solution(2651746282693253008)
XLA Ops:
  7.2 0.0 all-reduce.3.cloned.1.call-start
  7.2 0.0 copy-start
  7.2 12.5 %all_gather.3 = f32[128,1024]{1,0:T(8,128)S(1)} all-gather(f32[16,1024]{1,0:T(8,128)} %param.8), channel_id=1, replica_groups=mesh['gx'=8,'row'=4] {'gx'}, dimensions={0}, use_global_device_ids=true | all-gather | bytes 589824 | tf_op jit(solution)/shard_map/all_gather | solution.py:24
  19.8 0.9 fusion.4
  20.6 0.8 fusion.2
  21.5 0.6 mul.19
  22.1 0.0 copy-done
  22.1 0.0 copy-start.4
  22.1 0.0 copy-start.2
  22.2 0.0 copy-start.3
  22.2 0.0 copy-start.1
  22.2 7.2 %fusion = f32[2048,128]{0,1:T(8,128)S(1)} fusion(f32[128,1024]{1,0:T(8,128)S(1)} %all_gather.3, f32[1024,2048]{1,0:T(8,128)S(1)} %copy-done, f32[128,8,16,128]{3,2,1,0:T(8,128)S(1)} %bitcast.14), kind=kOutput, calls=%fused_computation.1 | convolution fusion | flops 3223322624 | bytes 18350080 | tf_op jit(solution)/shard_map/dot_general | solution.py:23
  29.4 17.9 %all_to_all.19 = f32[8,16,2048]{2,1,0:T(8,128)S(1)} all-to-all(f32[8,16,2048]{2,1,0:T(8,128)S(1)} %bitcast.15), channel_id=1, replica_groups=mesh['gx'=8,'row'=4] {'gx'}, dimensions={0} | all-to-all | bytes 2097152 | tf_op jit(solution)/shard_map/all_to_all | solution.py:29
  47.3 1.1 %copy.15 = f32[8,2,8,2048]{3,2,0,1:T(8,128)} copy(f32[8,2,8,2048]{3,2,1,0:T(8,128)S(1)} %bitcast.17) | data formatting | bytes 2097152 | tf_op jit(solution)/shard_map/all_to_all | solution.py:29
  48.4 0.0 all-reduce.3.cloned.1.call-update
  48.4 0.0 copy-done.4
  48.4 0.6 dynamic-slice
  49.7 0.0 copy-done.2
  49.7 0.0 copy-done.3
  49.7 0.2 select_reduce_fusion
  49.9 50.0 %all-reduce.3.cloned.1.call-done = f32[16,16384]{1,0:T(8,128)} async-done(((f32[16,16384]{1,0:T(8,128)}), f32[16,16384]{1,0:T(8,128)}) %all-reduce.3.cloned.1.call-update) | async-done | bytes 1048592
  99.8 0.0 copy-done.1
  99.8 1.9 %subtract_divide_fusion = (f32[4,16384]{1,0:T(4,128)}, f32[4,16384]{1,0:T(4,128)}) fusion(f32[4]{0:T(128)S(1)} %select_reduce_fusion, f32[16384]{0:T(1024)S(1)} %copy-done.1, f32[16,16384]{1,0:T(8,128)} %all-reduce.3.cloned.1.call-done, u32[]{:T(128)S(6)} %multiply.1), kind=kLoop, calls=%fused_computation.3 | loop fusion | flops 131072 | bytes 851988 | tf_op jit(solution)/shard_map/div | solution.py:34
Async XLA Ops:
  7.2 92.7 %all-reduce.3.cloned.1.call-start = ((), (), s32[]{:S(2)}) async-start(), calls=%async_computation.1 | async-start | bytes 2097152
  7.2 14.9 %copy-start = (f32[1024,2048]{1,0:T(8,128)S(1)}, f32[1024,2048]{1,0:T(8,128)}, u32[]{:S(2)}) copy-start(f32[1024,2048]{1,0:T(8,128)} %param.9) | copy-start | bytes 25165828
  22.1 26.3 %copy-start.4 = (u32[32]{0:T(128)S(1)}, u32[32]{0:T(128)}, u32[]{:S(2)}) copy-start(u32[32]{0:T(128)} %constant.6) | copy-start | bytes 388
  22.1 27.5 %copy-start.2 = (s32[4,2]{0,1:T(2,128)S(1)}, s32[4,2]{0,1:T(2,128)}, u32[]{:S(2)}) copy-start(s32[4,2]{0,1:T(2,128)} %param.13) | copy-start | bytes 100
  22.2 27.5 %copy-start.3 = (f32[100]{0:T(128)S(1)}, f32[100]{0:T(128)}, u32[]{:S(2)}) copy-start(f32[100]{0:T(128)} %param.14) | copy-start | bytes 1204
  22.2 77.7 %copy-start.1 = (f32[16384]{0:T(1024)S(1)}, f32[16384]{0:T(1024)}, u32[]{:S(2)}) copy-start(f32[16384]{0:T(1024)} %param.15) | copy-start | bytes 196612
Sparse Core Ops, SparseCore 0:
  48.5 51.2 all-reduce.2
where the time goes:
time: 109 us
  waiting for transfers between devices  50 us (46%)
  blocking collectives  30.4 us (28%)
  between operations  14.8 us (14%)
  matrix products  8.95 us (8%)
  local copies, waits for them, and re-layouts  2.34 us (2%)
  other arithmetic  2.12 us (2%)
    unnamed x2, waiting for transfers between devices  50 us
    all_to_all x1, blocking collectives, body(): lax.all_to_all(partial_value, 'gx', split_axis=0, concat_axis=1, tiled=True)  17.9 us
    all_gather x1, blocking collectives, body(): lax.all_gather(amplitudes, 'gx', axis=0, tiled=True)  12.5 us
    dot_general x1, matrix products, body(): jnp.dot(lax.all_gather(amplitudes, 'gx', axis=0, tiled=True), effective,...  7.21 us
  transfers between devices with their start and end apart: 1, of which 1 were waited for; matrix products, arithmetic and copies ran while one was open for 1% of the time, Pallas kernels for 0%

commit v1 on v0

--- a/solution.py
+++ b/solution.py
@@ -1,12 +1,18 @@
+import functools
+
 import jax
 import jax.numpy as jnp
 from jax import lax
+from jax.experimental import pallas as pl
+from jax.experimental.pallas import tpu as pltpu
 from jax.sharding import PartitionSpec as P
 
 BLK = 128
-
-
-def body(amplitudes, integrals, cd_irrep, ab_irrep, allowed, pair_occ, occ_energy, ab_energy):
+MESH = pl.DeviceIdType.MESH
+VMEM_BUDGET = 48 * 2**20
+
+
+def plain_body(amplitudes, integrals, cd_irrep, ab_irrep, allowed, pair_occ, occ_energy, ab_energy):
     irrep_labels = jnp.arange(allowed.shape[0], dtype=jnp.int32)
     cd_onehot = (cd_irrep[:, None] == irrep_labels[None, :]).astype(jnp.float32)
     ab_onehot = (ab_irrep[:, None] == irrep_labels[None, :]).astype(jnp.float32)
@@ -35,7 +41,258 @@
     return (residual, update)
 
 
+def kernel(
+    N, Z, T, W,
+    amp, integ, cd, ab, allowed, pair_occ, occ, ab_energy,
+    res_out, upd_out,
+    raw, wh, wl, gathered, ordered, a2, own, arrive, fin, landed,
+    isem, ag_send, ag_recv, relay_send, zsend, zrecv, xsend, xrecv,
+):
+    g = lax.axis_index("gx")
+    z = lax.axis_index("row")
+    rows, K = amp.shape
+    PP = rows * N
+    pk = rows // Z
+    partner = g + 1 - 2 * lax.rem(g, 2)
+    parity = lax.rem(g, 2)
+
+    def load(t):
+        cols = pl.ds(pl.multiple_of(t * W, W), W)
+        return pltpu.make_async_copy(integ.at[:, cols], raw.at[t], isem.at[t])
+
+    for t in range(T):
+        load(t).start()
+
+    barrier = pltpu.get_barrier_semaphore()
+    for j in range(1, N):
+        pl.semaphore_signal(barrier, inc=1, device_id={"gx": lax.rem(g + j, N)}, device_id_type=MESH)
+
+    @pl.when(z > 0)
+    def _():
+        pl.semaphore_signal(barrier, inc=1, device_id={"row": z - 1}, device_id_type=MESH)
+
+    @pl.when(z < Z - 1)
+    def _():
+        pl.semaphore_signal(barrier, inc=1, device_id={"row": z + 1}, device_id_type=MESH)
+
+    nearby = jnp.where(z > 0, 1, 0) + jnp.where(z < Z - 1, 1, 0)
+    pl.semaphore_wait(barrier, N - 1 + nearby)
+
+    def send_own(peer):
+        return pltpu.make_async_remote_copy(
+            src_ref=amp, dst_ref=gathered.at[g], send_sem=ag_send.at[peer], recv_sem=ag_recv.at[g],
+            device_id={"gx": peer}, device_id_type=MESH)
+
+    def relay(s):
+        return pltpu.make_async_remote_copy(
+            src_ref=gathered.at[s], dst_ref=gathered.at[s], send_sem=relay_send.at[s], recv_sem=ag_recv.at[s],
+            device_id={"gx": partner}, device_id_type=MESH)
+
+    like = [lax.rem(g + 2 * j, N) for j in range(N // 2 - 1, 0, -1)]
+    for peer in like:
+        send_own(peer).start()
+    send_own(partner).start()
+    gathered[g] = amp[...]
+
+    KB = K // BLK
+    WB = W // BLK
+
+    def split(t, carry):
+        load(t).wait()
+        for b in range(KB):
+            for j in range(WB):
+                m = allowed[cd[b], ab[t * WB + j]].astype(jnp.float32)
+                x = raw[t, b * BLK:(b + 1) * BLK, j * BLK:(j + 1) * BLK] * m
+                hi = x.astype(jnp.bfloat16)
+                wh[t, b * BLK:(b + 1) * BLK, j * BLK:(j + 1) * BLK] = hi
+                wl[t, b * BLK:(b + 1) * BLK, j * BLK:(j + 1) * BLK] = (x - hi.astype(jnp.float32)).astype(jnp.bfloat16)
+        return carry
+
+    lax.fori_loop(0, T, split, 0)
+
+    for s in like[::-1]:
+        relay(s).wait_recv()
+        relay(s).start()
+    relay(partner).wait_recv()
+    for j in range(1, N // 2):
+        relay(lax.rem(partner + 2 * j, N)).wait_recv()
+
+    for r in range(Z):
+        for s in range(N):
+            at = r * N * pk + s * pk
+            ordered[at:at + pk, :] = gathered[s, r * pk:(r + 1) * pk, :]
+    x = ordered[...]
+    hi = x.astype(jnp.bfloat16)
+    a2[0:PP, :] = hi
+    a2[PP:2 * PP, :] = (x - hi.astype(jnp.float32)).astype(jnp.bfloat16)
+
+    RP = N * pk
+
+    def send_z(d, t, up):
+        to = z + 1 if up else z - 1
+        side = 0 if up else 1
+        return pltpu.make_async_remote_copy(
+            src_ref=own.at[d, t], dst_ref=arrive.at[side, d, t], send_sem=zsend.at[d, t],
+            recv_sem=zrecv.at[side, d, t], device_id={"row": to}, device_id_type=MESH)
+
+    def compute(t, carry):
+        both = jnp.dot(a2[...], wh[t], preferred_element_type=jnp.float32)
+        tail = jnp.dot(a2[0:PP, :], wl[t], preferred_element_type=jnp.float32)
+        total = both[0:PP] + both[PP:2 * PP] + tail
+        for d in range(Z):
+            own[d, t] = total[d * RP:(d + 1) * RP, :]
+
+        @pl.when(z == 0)
+        def _():
+            send_z(Z - 1, t, True).start()
+
+        @pl.when(z == Z - 1)
+        def _():
+            send_z(0, t, False).start()
+        return carry
+
+    lax.fori_loop(0, T, compute, 0)
+
+    def pass_on(d, t, up):
+        side = 0 if up else 1
+        send_z(d, t, up).wait_recv()
+        own[d, t] = own[d, t] + arrive[side, d, t]
+
+    for i in range(Z - 1):
+        du, dd = Z - 1 - i, i
+
+        def step(t, carry):
+            @pl.when(jnp.logical_and(z > 0, z < du))
+            def _():
+                pass_on(du, t, True)
+
+            @pl.when(jnp.logical_and(z < du, z > (0 if i == 0 else -1)))
+            def _():
+                send_z(du, t, True).start()
+
+            @pl.when(jnp.logical_and(z < Z - 1, z > dd))
+            def _():
+                pass_on(dd, t, False)
+
+            @pl.when(jnp.logical_and(z > dd, z < (Z - 1 if i == 0 else Z)))
+            def _():
+                send_z(dd, t, False).start()
+            return carry
+
+        lax.fori_loop(0, T, step, 0)
+
+    def to_peer(peer, t):
+        return pltpu.make_async_remote_copy(
+            src_ref=fin.at[peer, t], dst_ref=landed.at[g, t], send_sem=xsend.at[peer], recv_sem=xrecv.at[g],
+            device_id={"gx": peer}, device_id_type=MESH)
+
+    def close(t, carry):
+        @pl.when(z > 0)
+        def _():
+            pass_on(z, t, True)
+
+        @pl.when(z < Z - 1)
+        def _():
+            pass_on(z, t, False)
+
+        total = own[z, t]
+        for s in range(N):
+            fin[s, t] = total[s * pk:(s + 1) * pk, :]
+        for j in range(1, N):
+            to_peer(lax.rem(g + j, N), t).start()
+        return carry
+
+    lax.fori_loop(0, T, close, 0)
+
+    pair = [occ[pair_occ[k, 0]] + occ[pair_occ[k, 1]] for k in range(pk)]
+    which = lax.broadcasted_iota(jnp.int32, (pk, W), 0)
+    pe = jnp.zeros((pk, W), jnp.float32)
+    for k in range(pk):
+        pe = jnp.where(which == k, pair[k], pe)
+
+    def finish(src, at):
+        for t in range(T):
+            cols = pl.ds(pl.multiple_of((at * T + t) * W, W), W)
+            v = src[at, t]
+            res_out[:, cols] = v
+            upd_out[:, cols] = v / (ab_energy[:, cols] - pe)
+
+    def whole(s):
+        return pltpu.make_async_remote_copy(
+            src_ref=fin.at[s], dst_ref=landed.at[s], send_sem=xsend.at[s], recv_sem=xrecv.at[s],
+            device_id={"gx": s}, device_id_type=MESH)
+
+    finish(fin, g)
+
+    def collect(j, carry):
+        s = lax.rem(g + j, N)
+        whole(s).wait_recv()
+        finish(landed, s)
+        return carry
+
+    lax.fori_loop(1, N, collect, 0)
+
+    for peer in like:
+        send_own(peer).wait_send()
+        relay(peer).wait_send()
+    send_own(partner).wait_send()
+
+    def drain(j, carry):
+        whole(lax.rem(g + j, N)).wait_send()
+        return carry
+
+    lax.fori_loop(1, N, drain, 0)
+    for d in range(Z):
+        @pl.when(z != d)
+        def _():
+            def drain_z(t, carry):
+                send_z(d, t, True).wait_send()
+                return carry
+            lax.fori_loop(0, T, drain_z, 0)
+
+
+def fused_body(N, Z, W, amplitudes, integrals, cd_irrep, ab_irrep, allowed, pair_occ, occ_energy, ab_energy):
+    rows, K = amplitudes.shape
+    AB = integrals.shape[1]
+    A = ab_energy.shape[0]
+    T = AB // W
+    pk = rows // Z
+    RP = N * pk
+    PP = rows * N
+    vmem, smem, hbm = pltpu.VMEM, pltpu.SMEM, pl.ANY
+    f32, bf16 = jnp.float32, jnp.bfloat16
+    dma = pltpu.SemaphoreType.DMA
+    out = jax.ShapeDtypeStruct((pk, A), f32)
+    return pl.pallas_call(
+        functools.partial(kernel, N, Z, T, W),
+        out_shape=(out, out),
+        in_specs=[pl.BlockSpec(memory_space=s) for s in (vmem, hbm, smem, smem, smem, smem, smem, vmem)],
+        out_specs=[pl.BlockSpec(memory_space=vmem)] * 2,
+        scratch_shapes=[
+            vmem((T, K, W), f32), vmem((T, K, W), bf16), vmem((T, K, W), bf16),
+            vmem((N, rows, K), f32), vmem((PP, K), f32), vmem((2 * PP, K), bf16),
+            vmem((Z, T, RP, W), f32), vmem((2, Z, T, RP, W), f32),
+            vmem((N, T, pk, W), f32), vmem((N, T, pk, W), f32),
+            dma((T,)), dma((N,)), dma((N,)), dma((N,)), dma((Z, T)), dma((2, Z, T)), dma((N,)), dma((N,)),
+        ],
+        compiler_params=pltpu.CompilerParams(
+            collective_id=0, has_side_effects=True, vmem_limit_bytes=VMEM_BUDGET),
+    )(amplitudes, integrals, cd_irrep, ab_irrep, allowed, pair_occ, occ_energy, ab_energy.reshape(1, A))
+
+
 def solution(mesh):
+    N, Z = mesh.shape["gx"], mesh.shape["row"]
+
+    def body(amplitudes, integrals, *rest):
+        rows, K = amplitudes.shape
+        AB = integrals.shape[1]
+        W = 2 * BLK
+        pk = rows // Z
+        need = 8 * K * AB + 16 * rows * N * K + 12 * rows * N * AB + 24 * pk * AB * N
+        if need > VMEM_BUDGET * 3 // 4 or AB % W or N % 2 or rows % Z:
+            return plain_body(amplitudes, integrals, *rest)
+        return fused_body(N, Z, W, amplitudes, integrals, *rest)
+
     return jax.shard_map(
         body,
         mesh=mesh,

time: 109 us -> 75.4 us (0.69)
  the two profiles are of different devices: /device:TPU:0 before, /device:TPU:17 now
where the time goes in v1:
time: 75.4 us; the launch traced here: 75.2 us
  Pallas kernels  68 us (90%)
  local copies, waits for them, and re-layouts  6.5 us (9%)
    pallas_call x1, Pallas kernels, fused_body(): pl.pallas_call(functools.partial(kernel, N, Z, T, W), out_shape=(out, out...  68 us
    unnamed x15, local copies, waits for them, and re-layouts  6.5 us

profile of v1, /device:TPU:17, one launch (start us, length us, event | category | flops | bytes accessed | tf_op | source)
XLA Modules:
  0.0 75.2 jit_solution(6949740579487452351)
XLA Ops:
  0.6 0.8 %copy.10.pair_occ = s32[4,2]{1,0:T(4,128)S(1)} copy(s32[4,2]{0,1:T(2,128)} %param.13) | data formatting | bytes 64 | tf_op args[5]
  1.4 0.0 copy-start
  1.4 0.8 %copy-done = f32[16,1024]{1,0:T(8,128)S(1)} copy-done((f32[16,1024]{1,0:T(8,128)S(1)}, f32[16,1024]{1,0:T(8,128)}, u32[]{:S(2)}) %copy-start) | copy-done | bytes 65560
  2.2 0.0 copy-start.1
  2.2 0.8 %copy-done.1 = f32[16384]{0:T(1024)S(1)} copy-done((f32[16384]{0:T(1024)S(1)}, f32[16384]{0:T(1024)}, u32[]{:S(2)}) %copy-start.1) | copy-done | bytes 65560
  3.1 0.0 copy-start.2
  3.1 0.7 copy-done.2
  3.8 0.0 copy-start.3
  3.8 0.7 copy-done.3
  4.4 0.0 copy-start.4
  4.4 0.7 copy-done.4
  5.1 0.0 copy-start.5
  5.1 0.7 copy-done.5
  5.7 68.0 %shard_map.95 = (f32[4,16384]{1,0:T(4,128)S(1)}, f32[4,16384]{1,0:T(4,128)S(1)}) custom-call(f32[16,1024]{1,0:T(8,128)S(1)} %copy-done, f32[1024,2048]{1,0:T(8,128)} %integ.1, s32[8]{0:T(128)S(1)} %copy-done.3, s32[16]{0:T(128)S(1)} %copy-done.4, s32[8,8]{1,0:T(8,128)S(1)} %copy-done.2, s32[4,2]{1,0:T(4,128)S(1)} %copy.10.pair_occ, f32[100]{0:T(128)S(1)} %copy-done.5, ...), custom_call_target="tpu_custom_call" | custom-call | tf_op jit(solution)/shard_map/pallas_call | solution.py:266
  73.7 0.7 copy.13
  74.5 0.7 copy.14
Async XLA Ops:
  1.4 0.8 %copy-start = (f32[16,1024]{1,0:T(8,128)S(1)}, f32[16,1024]{1,0:T(8,128)}, u32[]{:S(2)}) copy-start(f32[16,1024]{1,0:T(8,128)} %amp.1) | copy-start | bytes 196612
  2.2 0.8 %copy-start.1 = (f32[16384]{0:T(1024)S(1)}, f32[16384]{0:T(1024)}, u32[]{:S(2)}) copy-start(f32[16384]{0:T(1024)} %param.15) | copy-start | bytes 196612
  3.1 0.7 copy-start.2
  3.8 0.7 copy-start.3
  4.4 0.7 copy-start.4
  5.1 0.7 copy-start.5

commit v2 on v1

--- a/solution.py
+++ b/solution.py
@@ -10,6 +10,7 @@
 BLK = 128
 MESH = pl.DeviceIdType.MESH
 VMEM_BUDGET = 48 * 2**20
+VMEM_GRANT = 67043328
 
 
 def plain_body(amplitudes, integrals, cd_irrep, ab_irrep, allowed, pair_occ, occ_energy, ab_energy):
@@ -42,9 +43,10 @@
 
 
 def kernel(
-    N, Z, T, W,
-    amp, integ, cd, ab, allowed, pair_occ, occ, ab_energy,
+    N, Z, T, W, L,
+    amp, integ, cd_in, ab_in, allowed_in, pair_in, occ_in, energy_in,
     res_out, upd_out,
+    cd, ab, allowed, pair_occ, occ, ab_energy, small_sem, amp_sem,
     raw, wh, wl, gathered, ordered, a2, own, arrive, fin, landed,
     isem, ag_send, ag_recv, relay_send, zsend, zrecv, xsend, xrecv,
 ):
@@ -60,6 +62,15 @@
         cols = pl.ds(pl.multiple_of(t * W, W), W)
         return pltpu.make_async_copy(integ.at[:, cols], raw.at[t], isem.at[t])
 
+    own_amp = pltpu.make_async_copy(amp, gathered.at[g], amp_sem)
+    own_amp.start()
+    small = [
+        pltpu.make_async_copy(src, dst, small_sem.at[i])
+        for i, (src, dst) in enumerate((
+            (cd_in, cd), (ab_in, ab), (allowed_in, allowed), (pair_in, pair_occ), (occ_in, occ), (energy_in, ab_energy)))
+    ]
+    for c in small:
+        c.start()
     for t in range(T):
         load(t).start()
 
@@ -80,7 +91,7 @@
 
     def send_own(peer):
         return pltpu.make_async_remote_copy(
-            src_ref=amp, dst_ref=gathered.at[g], send_sem=ag_send.at[peer], recv_sem=ag_recv.at[g],
+            src_ref=gathered.at[g], dst_ref=gathered.at[g], send_sem=ag_send.at[peer], recv_sem=ag_recv.at[g],
             device_id={"gx": peer}, device_id_type=MESH)
 
     def relay(s):
@@ -89,10 +100,12 @@
             device_id={"gx": partner}, device_id_type=MESH)
 
     like = [lax.rem(g + 2 * j, N) for j in range(N // 2 - 1, 0, -1)]
+    own_amp.wait()
     for peer in like:
         send_own(peer).start()
     send_own(partner).start()
-    gathered[g] = amp[...]
+    for c in small:
+        c.wait()
 
     KB = K // BLK
     WB = W // BLK
@@ -135,76 +148,82 @@
             src_ref=own.at[d, t], dst_ref=arrive.at[side, d, t], send_sem=zsend.at[d, t],
             recv_sem=zrecv.at[side, d, t], device_id={"row": to}, device_id_type=MESH)
 
-    def compute(t, carry):
+    def compute(t):
         both = jnp.dot(a2[...], wh[t], preferred_element_type=jnp.float32)
         tail = jnp.dot(a2[0:PP, :], wl[t], preferred_element_type=jnp.float32)
         total = both[0:PP] + both[PP:2 * PP] + tail
         for d in range(Z):
             own[d, t] = total[d * RP:(d + 1) * RP, :]
 
-        @pl.when(z == 0)
-        def _():
-            send_z(Z - 1, t, True).start()
-
-        @pl.when(z == Z - 1)
-        def _():
-            send_z(0, t, False).start()
-        return carry
-
-    lax.fori_loop(0, T, compute, 0)
-
-    def pass_on(d, t, up):
+    def take(d, t, up):
         side = 0 if up else 1
         send_z(d, t, up).wait_recv()
         own[d, t] = own[d, t] + arrive[side, d, t]
 
-    for i in range(Z - 1):
-        du, dd = Z - 1 - i, i
-
-        def step(t, carry):
-            @pl.when(jnp.logical_and(z > 0, z < du))
-            def _():
-                pass_on(du, t, True)
-
-            @pl.when(jnp.logical_and(z < du, z > (0 if i == 0 else -1)))
-            def _():
-                send_z(du, t, True).start()
-
-            @pl.when(jnp.logical_and(z < Z - 1, z > dd))
-            def _():
-                pass_on(dd, t, False)
-
-            @pl.when(jnp.logical_and(z > dd, z < (Z - 1 if i == 0 else Z)))
-            def _():
-                send_z(dd, t, False).start()
-            return carry
-
-        lax.fori_loop(0, T, step, 0)
-
     def to_peer(peer, t):
         return pltpu.make_async_remote_copy(
             src_ref=fin.at[peer, t], dst_ref=landed.at[g, t], send_sem=xsend.at[peer], recv_sem=xrecv.at[g],
             device_id={"gx": peer}, device_id_type=MESH)
 
-    def close(t, carry):
+    def close(t):
         @pl.when(z > 0)
         def _():
-            pass_on(z, t, True)
+            take(z, t, True)
 
         @pl.when(z < Z - 1)
         def _():
-            pass_on(z, t, False)
+            take(z, t, False)
 
         total = own[z, t]
         for s in range(N):
             fin[s, t] = total[s * pk:(s + 1) * pk, :]
         for j in range(1, N):
             to_peer(lax.rem(g + j, N), t).start()
+
+    last = Z - 1 - z
+    lag_up, lag_down = z * L, last * L
+    first_close = jnp.maximum(last * T + lag_up, z * T + lag_down)
+
+    def step(s, carry):
+        @pl.when(s < T)
+        def _():
+            compute(s)
+
+        qu = s - lag_up
+
+        @pl.when(jnp.logical_and(qu >= 0, qu < last * T))
+        def _():
+            d, t = Z - 1 - qu // T, lax.rem(qu, T)
+
+            @pl.when(z > 0)
+            def _():
+                take(d, t, True)
+
+            send_z(d, t, True).start()
+
+        qd = s - lag_down
+
+        @pl.when(jnp.logical_and(qd >= 0, qd < z * T))
+        def _():
+            d, t = qd // T, lax.rem(qd, T)
+
+            @pl.when(z < Z - 1)
+            def _():
+                take(d, t, False)
+
+            send_z(d, t, False).start()
+
+        tc = s - first_close
+
+        @pl.when(jnp.logical_and(tc >= 0, tc < T))
+        def _():
+            close(tc)
+
         return carry
 
-    lax.fori_loop(0, T, close, 0)
-
-    pair = [occ[pair_occ[k, 0]] + occ[pair_occ[k, 1]] for k in range(pk)]
+    lax.fori_loop(0, Z * T + (Z - 1) * L, step, 0)
+
+    pair = [occ[pair_occ[0, k]] + occ[pair_occ[1, k]] for k in range(pk)]
     which = lax.broadcasted_iota(jnp.int32, (pk, W), 0)
     pe = jnp.zeros((pk, W), jnp.float32)
     for k in range(pk):
@@ -251,7 +270,7 @@
             lax.fori_loop(0, T, drain_z, 0)
 
 
-def fused_body(N, Z, W, amplitudes, integrals, cd_irrep, ab_irrep, allowed, pair_occ, occ_energy, ab_energy):
+def fused_body(N, Z, W, L, amplitudes, integrals, cd_irrep, ab_irrep, allowed, pair_occ, occ_energy, ab_energy):
     rows, K = amplitudes.shape
     AB = integrals.shape[1]
     A = ab_energy.shape[0]
@@ -259,16 +278,18 @@
     pk = rows // Z
     RP = N * pk
     PP = rows * N
-    vmem, smem, hbm = pltpu.VMEM, pltpu.SMEM, pl.ANY
-    f32, bf16 = jnp.float32, jnp.bfloat16
+    vmem, smem = pltpu.VMEM, pltpu.SMEM
+    f32, bf16, i32 = jnp.float32, jnp.bfloat16, jnp.int32
     dma = pltpu.SemaphoreType.DMA
     out = jax.ShapeDtypeStruct((pk, A), f32)
     return pl.pallas_call(
-        functools.partial(kernel, N, Z, T, W),
+        functools.partial(kernel, N, Z, T, W, L),
         out_shape=(out, out),
-        in_specs=[pl.BlockSpec(memory_space=s) for s in (vmem, hbm, smem, smem, smem, smem, smem, vmem)],
+        in_specs=[pl.BlockSpec(memory_space=pltpu.HBM)] * 8,
         out_specs=[pl.BlockSpec(memory_space=vmem)] * 2,
         scratch_shapes=[
+            smem(cd_irrep.shape, i32), smem(ab_irrep.shape, i32), smem(allowed.shape, i32),
+            smem(pair_occ.shape[::-1], i32), smem(occ_energy.shape, f32), vmem((1, A), f32), dma((6,)), dma,
             vmem((T, K, W), f32), vmem((T, K, W), bf16), vmem((T, K, W), bf16),
             vmem((N, rows, K), f32), vmem((PP, K), f32), vmem((2 * PP, K), bf16),
             vmem((Z, T, RP, W), f32), vmem((2, Z, T, RP, W), f32),
@@ -276,8 +297,8 @@
             dma((T,)), dma((N,)), dma((N,)), dma((N,)), dma((Z, T)), dma((2, Z, T)), dma((N,)), dma((N,)),
         ],
         compiler_params=pltpu.CompilerParams(
-            collective_id=0, has_side_effects=True, vmem_limit_bytes=VMEM_BUDGET),
-    )(amplitudes, integrals, cd_irrep, ab_irrep, allowed, pair_occ, occ_energy, ab_energy.reshape(1, A))
+            collective_id=0, has_side_effects=True, vmem_limit_bytes=VMEM_GRANT),
+    )(amplitudes, integrals, cd_irrep, ab_irrep, allowed, pair_occ.T, occ_energy, ab_energy.reshape(1, A))
 
 
 def solution(mesh):
@@ -291,7 +312,7 @@
         need = 8 * K * AB + 16 * rows * N * K + 12 * rows * N * AB + 24 * pk * AB * N
         if need > VMEM_BUDGET * 3 // 4 or AB % W or N % 2 or rows % Z:
             return plain_body(amplitudes, integrals, *rest)
-        return fused_body(N, Z, W, amplitudes, integrals, *rest)
+        return fused_body(N, Z, W, 3, amplitudes, integrals, *rest)
 
     return jax.shard_map(
         body,

time: 75.4 us -> 39.8 us (0.53)
  Pallas kernels: 68 us -> 35.6 us
  local copies, waits for them, and re-layouts: 6.5 us -> 3.34 us
    pallas_call x1, Pallas kernels: 68 us -> 35.6 us  [fused_body(): pl.pallas_call(functools.partial(kernel, N, Z, T, W, L), out_shape=(out,...]
    unnamed x15 -> x2, local copies, waits for them, and re-layouts: 6.5 us -> 3.34 us
where the time goes in v2:
time: 39.8 us; the launch traced here: 39.6 us
  Pallas kernels  35.6 us (89%)
  local copies, waits for them, and re-layouts  3.34 us (8%)
  between operations  0.64 us (2%)
    pallas_call x1, Pallas kernels, fused_body(): pl.pallas_call(functools.partial(kernel, N, Z, T, W, L), out_shape=(out,...  35.6 us
    unnamed x2, local copies, waits for them, and re-layouts  3.34 us

profile of v2, /device:TPU:17, one launch (start us, length us, event | category | flops | bytes accessed | tf_op | source)
XLA Modules:
  0.0 39.6 jit_solution(1523471576761941890)
XLA Ops:
  0.6 35.6 %shard_map.95 = (f32[4,16384]{1,0:T(4,128)}, f32[4,16384]{1,0:T(4,128)}) custom-call(f32[16,1024]{1,0:T(8,128)} %amp.1, f32[1024,2048]{1,0:T(8,128)} %integ.1, s32[8]{0:T(128)} %cd_in.1, s32[16]{0:T(128)} %ab_in.1, s32[8,8]{1,0:T(8,128)} %allowed_in.1, s32[2,4]{1,0:T(2,128)} %bitcast.3, f32[100]{0:T(128)} %occ_in.1, f32[1,16384]{1,0:T(1,128)} %bitcast.2), custom_call_target="tpu_custom_call" | custom-call | tf_op jit(solution)/shard_map/pallas_call | solution.py:285
  36.2 1.7 %copy.12 = f32[4,16384]{1,0:T(4,128)} copy(f32[4,16384]{1,0:T(4,128)} %get-tuple-element.4) | data formatting | bytes 524288
  37.9 1.7 %copy.13 = f32[4,16384]{1,0:T(4,128)} copy(f32[4,16384]{1,0:T(4,128)} %get-tuple-element.5) | data formatting | bytes 524288

commit v3 on v2

--- a/solution.py
+++ b/solution.py
@@ -44,17 +44,19 @@
 
 def kernel(
     N, Z, T, W, L,
-    amp, integ, cd_in, ab_in, allowed_in, pair_in, occ_in, energy_in,
-    res_out, upd_out,
-    cd, ab, allowed, pair_occ, occ, ab_energy, small_sem, amp_sem,
-    raw, wh, wl, gathered, ordered, a2, own, arrive, fin, landed,
-    isem, ag_send, ag_recv, relay_send, zsend, zrecv, xsend, xrecv,
+    amp, integ, cd_in, ab_in, allowed_in,
+    res_out,
+    cd, ab, allowed, small_sem, amp_sem,
+    raw, wh, wl, gathered, ordered, a2, own, arrive, fin,
+    isem, ag_send, ag_recv, relay_send, zsend, zrecv, xsend, xrecv, own_sem,
 ):
     g = lax.axis_index("gx")
     z = lax.axis_index("row")
     rows, K = amp.shape
-    PP = rows * N
+    half, Zh = rows // 2, Z // 2
+    HP = half * N
     pk = rows // Z
+    far = jnp.where(z < Zh, 1, 0)
     partner = g + 1 - 2 * lax.rem(g, 2)
     parity = lax.rem(g, 2)
 
@@ -62,12 +64,16 @@
         cols = pl.ds(pl.multiple_of(t * W, W), W)
         return pltpu.make_async_copy(integ.at[:, cols], raw.at[t], isem.at[t])
 
-    own_amp = pltpu.make_async_copy(amp, gathered.at[g], amp_sem)
-    own_amp.start()
+    def own_amp(h):
+        return pltpu.make_async_copy(
+            amp.at[pl.ds(pl.multiple_of(h * half, half), half), :], gathered.at[g, h], amp_sem.at[h])
+
+    own_amp(far).start()
+    own_amp(1 - far).start()
     small = [
         pltpu.make_async_copy(src, dst, small_sem.at[i])
         for i, (src, dst) in enumerate((
-            (cd_in, cd), (ab_in, ab), (allowed_in, allowed), (pair_in, pair_occ), (occ_in, occ), (energy_in, ab_energy)))
+            (cd_in, cd), (ab_in, ab), (allowed_in, allowed)))
     ]
     for c in small:
         c.start()
@@ -89,21 +95,22 @@
     nearby = jnp.where(z > 0, 1, 0) + jnp.where(z < Z - 1, 1, 0)
     pl.semaphore_wait(barrier, N - 1 + nearby)
 
-    def send_own(peer):
-        return pltpu.make_async_remote_copy(
-            src_ref=gathered.at[g], dst_ref=gathered.at[g], send_sem=ag_send.at[peer], recv_sem=ag_recv.at[g],
-            device_id={"gx": peer}, device_id_type=MESH)
-
-    def relay(s):
-        return pltpu.make_async_remote_copy(
-            src_ref=gathered.at[s], dst_ref=gathered.at[s], send_sem=relay_send.at[s], recv_sem=ag_recv.at[s],
-            device_id={"gx": partner}, device_id_type=MESH)
+    def send_own(peer, h):
+        return pltpu.make_async_remote_copy(
+            src_ref=gathered.at[g, h], dst_ref=gathered.at[g, h], send_sem=ag_send.at[h, peer],
+            recv_sem=ag_recv.at[h, g], device_id={"gx": peer}, device_id_type=MESH)
+
+    def relay(s, h):
+        return pltpu.make_async_remote_copy(
+            src_ref=gathered.at[s, h], dst_ref=gathered.at[s, h], send_sem=relay_send.at[h, s],
+            recv_sem=ag_recv.at[h, s], device_id={"gx": partner}, device_id_type=MESH)
 
     like = [lax.rem(g + 2 * j, N) for j in range(N // 2 - 1, 0, -1)]
-    own_amp.wait()
-    for peer in like:
-        send_own(peer).start()
-    send_own(partner).start()
+    for h in (far, 1 - far):
+        own_amp(h).wait()
+        for peer in like:
+            send_own(peer, h).start()
+        send_own(partner, h).start()
     for c in small:
         c.wait()
 
@@ -123,21 +130,26 @@
 
     lax.fori_loop(0, T, split, 0)
 
-    for s in like[::-1]:
-        relay(s).wait_recv()
-        relay(s).start()
-    relay(partner).wait_recv()
-    for j in range(1, N // 2):
-        relay(lax.rem(partner + 2 * j, N)).wait_recv()
-
-    for r in range(Z):
-        for s in range(N):
-            at = r * N * pk + s * pk
-            ordered[at:at + pk, :] = gathered[s, r * pk:(r + 1) * pk, :]
-    x = ordered[...]
-    hi = x.astype(jnp.bfloat16)
-    a2[0:PP, :] = hi
-    a2[PP:2 * PP, :] = (x - hi.astype(jnp.float32)).astype(jnp.bfloat16)
+    def forward(h):
+        for s in like[::-1]:
+            relay(s, h).wait_recv()
+            relay(s, h).start()
+
+    def prepare(h):
+        relay(partner, h).wait_recv()
+        for j in range(1, N // 2):
+            relay(lax.rem(partner + 2 * j, N), h).wait_recv()
+        for r in range(Zh):
+            for s in range(N):
+                at = (r * N + s) * pk
+                ordered[at:at + pk, :] = gathered[s, h, r * pk:(r + 1) * pk, :]
+        x = ordered[...]
+        hi = x.astype(jnp.bfloat16)
+        a2[0:HP, :] = hi
+        a2[HP:2 * HP, :] = (x - hi.astype(jnp.float32)).astype(jnp.bfloat16)
+
+    forward(far)
+    prepare(far)
 
     RP = N * pk
 
@@ -148,21 +160,27 @@
             src_ref=own.at[d, t], dst_ref=arrive.at[side, d, t], send_sem=zsend.at[d, t],
             recv_sem=zrecv.at[side, d, t], device_id={"row": to}, device_id_type=MESH)
 
-    def compute(t):
+    def compute(t, h):
         both = jnp.dot(a2[...], wh[t], preferred_element_type=jnp.float32)
-        tail = jnp.dot(a2[0:PP, :], wl[t], preferred_element_type=jnp.float32)
-        total = both[0:PP] + both[PP:2 * PP] + tail
-        for d in range(Z):
-            own[d, t] = total[d * RP:(d + 1) * RP, :]
+        tail = jnp.dot(a2[0:HP, :], wl[t], preferred_element_type=jnp.float32)
+        total = both[0:HP] + both[HP:2 * HP] + tail
+        for r in range(Zh):
+            own[h * Zh + r, t] = total[r * RP:(r + 1) * RP, :]
 
     def take(d, t, up):
         side = 0 if up else 1
         send_z(d, t, up).wait_recv()
         own[d, t] = own[d, t] + arrive[side, d, t]
 
+    def place(s, t):
+        return pl.ds(pl.multiple_of((s * T + t) * W, W), W)
+
+    def keep(t):
+        return pltpu.make_async_copy(fin.at[g, t], res_out.at[:, place(g, t)], own_sem.at[t])
+
     def to_peer(peer, t):
         return pltpu.make_async_remote_copy(
-            src_ref=fin.at[peer, t], dst_ref=landed.at[g, t], send_sem=xsend.at[peer], recv_sem=xrecv.at[g],
+            src_ref=fin.at[peer, t], dst_ref=res_out.at[:, place(g, t)], send_sem=xsend.at[peer], recv_sem=xrecv.at[g],
             device_id={"gx": peer}, device_id_type=MESH)
 
     def close(t):
@@ -179,15 +197,24 @@
             fin[s, t] = total[s * pk:(s + 1) * pk, :]
         for j in range(1, N):
             to_peer(lax.rem(g + j, N), t).start()
+        keep(t).start()
 
     last = Z - 1 - z
     lag_up, lag_down = z * L, last * L
     first_close = jnp.maximum(last * T + lag_up, z * T + lag_down)
 
     def step(s, carry):
-        @pl.when(s < T)
-        def _():
-            compute(s)
+        @pl.when(s == T // 4)
+        def _():
+            forward(1 - far)
+
+        @pl.when(s == T)
+        def _():
+            prepare(1 - far)
+
+        @pl.when(s < 2 * T)
+        def _():
+            compute(lax.rem(s, T), jnp.where(s < T, far, 1 - far))
 
         qu = s - lag_up
 
@@ -223,38 +250,30 @@
 
     lax.fori_loop(0, Z * T + (Z - 1) * L, step, 0)
 
-    pair = [occ[pair_occ[0, k]] + occ[pair_occ[1, k]] for k in range(pk)]
-    which = lax.broadcasted_iota(jnp.int32, (pk, W), 0)
-    pe = jnp.zeros((pk, W), jnp.float32)
-    for k in range(pk):
-        pe = jnp.where(which == k, pair[k], pe)
-
-    def finish(src, at):
-        for t in range(T):
-            cols = pl.ds(pl.multiple_of((at * T + t) * W, W), W)
-            v = src[at, t]
-            res_out[:, cols] = v
-            upd_out[:, cols] = v / (ab_energy[:, cols] - pe)
-
     def whole(s):
-        return pltpu.make_async_remote_copy(
-            src_ref=fin.at[s], dst_ref=landed.at[s], send_sem=xsend.at[s], recv_sem=xrecv.at[s],
+        band = res_out.at[:, pl.ds(pl.multiple_of(s * T * W, W), T * W)]
+        return pltpu.make_async_remote_copy(
+            src_ref=band, dst_ref=band, send_sem=xsend.at[s], recv_sem=xrecv.at[s],
             device_id={"gx": s}, device_id_type=MESH)
 
-    finish(fin, g)
+    for peer in like:
+        for h in range(2):
+            send_own(peer, h).wait_send()
+            relay(peer, h).wait_send()
+    for h in range(2):
+        send_own(partner, h).wait_send()
 
     def collect(j, carry):
-        s = lax.rem(g + j, N)
-        whole(s).wait_recv()
-        finish(landed, s)
+        whole(lax.rem(g + j, N)).wait_recv()
         return carry
 
     lax.fori_loop(1, N, collect, 0)
 
-    for peer in like:
-        send_own(peer).wait_send()
-        relay(peer).wait_send()
-    send_own(partner).wait_send()
+    def drain_own(t, carry):
+        keep(t).wait()
+        return carry
+
+    lax.fori_loop(0, T, drain_own, 0)
 
     def drain(j, carry):
         whole(lax.rem(g + j, N)).wait_send()
@@ -268,6 +287,17 @@
                 send_z(d, t, True).wait_send()
                 return carry
             lax.fori_loop(0, T, drain_z, 0)
+
+
+def divide(res, pair_occ, occ, energy, res_out, upd_out):
+    pk, A = res.shape
+    which = lax.broadcasted_iota(jnp.int32, (pk, 1), 0)
+    pe = jnp.zeros((pk, 1), jnp.float32)
+    for k in range(pk):
+        pe = jnp.where(which == k, occ[pair_occ[0, k]] + occ[pair_occ[1, k]], pe)
+    v = res[...]
+    res_out[...] = v
+    upd_out[...] = v / (energy[...] - pe)
 
 
 def fused_body(N, Z, W, L, amplitudes, integrals, cd_irrep, ab_irrep, allowed, pair_occ, occ_energy, ab_energy):
@@ -277,28 +307,34 @@
     T = AB // W
     pk = rows // Z
     RP = N * pk
-    PP = rows * N
+    HP = rows * N // 2
     vmem, smem = pltpu.VMEM, pltpu.SMEM
     f32, bf16, i32 = jnp.float32, jnp.bfloat16, jnp.int32
     dma = pltpu.SemaphoreType.DMA
     out = jax.ShapeDtypeStruct((pk, A), f32)
-    return pl.pallas_call(
+    residual = pl.pallas_call(
         functools.partial(kernel, N, Z, T, W, L),
-        out_shape=(out, out),
-        in_specs=[pl.BlockSpec(memory_space=pltpu.HBM)] * 8,
-        out_specs=[pl.BlockSpec(memory_space=vmem)] * 2,
+        out_shape=out,
+        in_specs=[pl.BlockSpec(memory_space=pltpu.HBM)] * 5,
+        out_specs=pl.BlockSpec(memory_space=pltpu.HBM),
         scratch_shapes=[
-            smem(cd_irrep.shape, i32), smem(ab_irrep.shape, i32), smem(allowed.shape, i32),
-            smem(pair_occ.shape[::-1], i32), smem(occ_energy.shape, f32), vmem((1, A), f32), dma((6,)), dma,
+            smem(cd_irrep.shape, i32), smem(ab_irrep.shape, i32), smem(allowed.shape, i32), dma((3,)), dma((2,)),
             vmem((T, K, W), f32), vmem((T, K, W), bf16), vmem((T, K, W), bf16),
-            vmem((N, rows, K), f32), vmem((PP, K), f32), vmem((2 * PP, K), bf16),
-            vmem((Z, T, RP, W), f32), vmem((2, Z, T, RP, W), f32),
-            vmem((N, T, pk, W), f32), vmem((N, T, pk, W), f32),
-            dma((T,)), dma((N,)), dma((N,)), dma((N,)), dma((Z, T)), dma((2, Z, T)), dma((N,)), dma((N,)),
+            vmem((N, 2, rows // 2, K), f32), vmem((HP, K), f32), vmem((2 * HP, K), bf16),
+            vmem((Z, T, RP, W), f32), vmem((2, Z, T, RP, W), f32), vmem((N, T, pk, W), f32),
+            dma((T,)), dma((2, N)), dma((2, N)), dma((2, N)), dma((Z, T)), dma((2, Z, T)), dma((N,)), dma((N,)),
+            dma((T,)),
         ],
         compiler_params=pltpu.CompilerParams(
             collective_id=0, has_side_effects=True, vmem_limit_bytes=VMEM_GRANT),
-    )(amplitudes, integrals, cd_irrep, ab_irrep, allowed, pair_occ.T, occ_energy, ab_energy.reshape(1, A))
+    )(amplitudes, integrals, cd_irrep, ab_irrep, allowed)
+    return pl.pallas_call(
+        divide,
+        out_shape=(out, out),
+        in_specs=[pl.BlockSpec(memory_space=s) for s in (vmem, smem, smem, vmem)],
+        out_specs=[pl.BlockSpec(memory_space=vmem)] * 2,
+        compiler_params=pltpu.CompilerParams(vmem_limit_bytes=VMEM_GRANT),
+    )(residual, pair_occ.T, occ_energy, ab_energy.reshape(1, A))
 
 
 def solution(mesh):
@@ -308,11 +344,12 @@
         rows, K = amplitudes.shape
         AB = integrals.shape[1]
         W = 2 * BLK
+        L = max(3, pl.cdiv(2 * (AB // W), Z))
         pk = rows // Z
         need = 8 * K * AB + 16 * rows * N * K + 12 * rows * N * AB + 24 * pk * AB * N
-        if need > VMEM_BUDGET * 3 // 4 or AB % W or N % 2 or rows % Z:
+        if need > VMEM_BUDGET * 3 // 4 or AB % W or N % 2 or Z % 2 or rows % Z or rows % 16:
             return plain_body(amplitudes, integrals, *rest)
-        return fused_body(N, Z, W, 3, amplitudes, integrals, *rest)
+        return fused_body(N, Z, W, L, amplitudes, integrals, *rest)
 
     return jax.shard_map(
         body,

time: 39.8 us -> 35.1 us (0.88)
  local copies, waits for them, and re-layouts: 3.34 us -> 0 us
  Pallas kernels: 35.6 us -> 34.3 us
    unnamed x2 -> x0, local copies, waits for them, and re-layouts: 3.34 us -> none
    pallas_call x1 -> x2, Pallas kernels: 35.6 us -> 34.3 us  [the longest x1 32.5 us: fused_body(): pl.pallas_call(functools.partial(kernel, N, Z, T, W, L), out_shape=out, i...]
where the time goes in v3:
time: 35.1 us; the launch traced here: 35 us
  Pallas kernels  34.3 us (98%)
  between operations  0.64 us (2%)
    pallas_call x1, Pallas kernels, fused_body(): pl.pallas_call(functools.partial(kernel, N, Z, T, W, L), out_shape=out, i...  32.5 us
    pallas_call x1, Pallas kernels, fused_body(): pl.pallas_call(divide, out_shape=(out, out), in_specs=[pl.BlockSpec(memor...  1.78 us

profile of v3, /device:TPU:17, one launch (start us, length us, event | category | flops | bytes accessed | tf_op | source)
XLA Modules:
  0.0 35.0 jit_solution(17315339133678027897)
XLA Ops:
  0.6 32.5 %shard_map.95.res = f32[4,16384]{1,0:T(4,128)} custom-call(f32[16,1024]{1,0:T(8,128)} %amp.1, f32[1024,2048]{1,0:T(8,128)} %integ.1, s32[8]{0:T(128)} %cd_in.1, s32[16]{0:T(128)} %ab_in.1, s32[8,8]{1,0:T(8,128)} %allowed_in.1), custom_call_target="tpu_custom_call" | custom-call | tf_op jit(solution)/shard_map/pallas_call | solution.py:315
  33.2 1.8 %shard_map.96 = (f32[4,16384]{1,0:T(4,128)}, f32[4,16384]{1,0:T(4,128)}) custom-call(f32[4,16384]{1,0:T(4,128)} %shard_map.95.res, s32[2,4]{1,0:T(2,128)} %bitcast.3, f32[100]{0:T(128)} %occ.1, f32[1,16384]{1,0:T(1,128)} %bitcast.2), custom_call_target="tpu_custom_call" | custom-call | tf_op jit(solution)/shard_map/pallas_call | solution.py:331

commit v4 on v3

--- a/solution.py
+++ b/solution.py
@@ -77,9 +77,6 @@
     ]
     for c in small:
         c.start()
-    for t in range(T):
-        load(t).start()
-
     barrier = pltpu.get_barrier_semaphore()
     for j in range(1, N):
         pl.semaphore_signal(barrier, inc=1, device_id={"gx": lax.rem(g + j, N)}, device_id_type=MESH)
@@ -111,6 +108,8 @@
         for peer in like:
             send_own(peer, h).start()
         send_own(partner, h).start()
+    for t in range(T):
+        load(t).start()
     for c in small:
         c.wait()
 

time: 35.1 us -> 34.4 us (0.980)
  Pallas kernels: 34.3 us -> 33.6 us
    pallas_call x1, Pallas kernels: 32.5 us -> 31.8 us  [fused_body(): pl.pallas_call(functools.partial(kernel, N, Z, T, W, L), out_shape=out, i...]
where the time goes in v4:
time: 34.4 us; the launch traced here: 34.2 us
  Pallas kernels  33.6 us (98%)
  between operations  0.64 us (2%)
    pallas_call x1, Pallas kernels, fused_body(): pl.pallas_call(functools.partial(kernel, N, Z, T, W, L), out_shape=out, i...  31.8 us
    pallas_call x1, Pallas kernels, fused_body(): pl.pallas_call(divide, out_shape=(out, out), in_specs=[pl.BlockSpec(memor...  1.78 us

profile of v4, /device:TPU:17, one launch (start us, length us, event | category | flops | bytes accessed | tf_op | source)
XLA Modules:
  0.0 34.2 jit_solution(4076760579978533054)
XLA Ops:
  0.6 31.8 %shard_map.95.res = f32[4,16384]{1,0:T(4,128)} custom-call(f32[16,1024]{1,0:T(8,128)} %amp.1, f32[1024,2048]{1,0:T(8,128)} %integ.1, s32[8]{0:T(128)} %cd_in.1, s32[16]{0:T(128)} %ab_in.1, s32[8,8]{1,0:T(8,128)} %allowed_in.1), custom_call_target="tpu_custom_call" | custom-call | tf_op jit(solution)/shard_map/pallas_call | solution.py:314
  32.5 1.8 %shard_map.96 = (f32[4,16384]{1,0:T(4,128)}, f32[4,16384]{1,0:T(4,128)}) custom-call(f32[4,16384]{1,0:T(4,128)} %shard_map.95.res, s32[2,4]{1,0:T(2,128)} %bitcast.3, f32[100]{0:T(128)} %occ.1, f32[1,16384]{1,0:T(1,128)} %bitcast.2), custom_call_target="tpu_custom_call" | custom-call | tf_op jit(solution)/shard_map/pallas_call | solution.py:330
